TPU v7x, 128 devices: a whole 4x4x4 slice. The times are simulated.
128 devices in a mesh: rep: 4 (over y), ep: 32 (over z, x, core).
Axes of the slice: x: 4, y: 4, z: 4, core: 2. Of those that a mesh axis runs over, the one named last changes fastest.
Arguments:
- tokens: bfloat16 [16384, 4096], P(('rep', 'ep')), may hold values from -6 to 6
- routes: int32 [16384, 8], P(('rep', 'ep')), may hold values from 0 to 31, as said below
- gate_scores: float32 [16384, 8], P(('rep', 'ep')), may hold values from 0.1 to 1
- slot_order: int32 [128, 128], P(('rep', 'ep')), may hold values from 0 to 127, each once within a row
- capacity: int32 [4, 32], replicated, may hold values from 384 to 1536, as said below
- w_gate: bfloat16 [32, 4096, 768], P('ep'), may hold values from -0.09375 to 0.09375
- w_up: bfloat16 [32, 4096, 768], P('ep'), may hold values from -0.09375 to 0.09375
- w_down: bfloat16 [32, 768, 4096], P('ep'), may hold values from -0.21875 to 0.21875
Outputs:
- mixed: bfloat16 [16384, 4096], P(('rep', 'ep'))
Inputs may be any that keep to these rules, and one draw needn't show every extreme that they name: `routes`: each row names 8 different experts; among the rows of one device no expert is named more than 40 times, and some device names some expert exactly 40 times. `slot_order`: each device's row is a permutation; a smaller value is served earlier. `capacity`: some entry equals 1536 and some equals 384.
All inputs are finite; a program needn't handle non-finite values.
Results may differ from a plain program's by a relative error of at most 0.0058.
Values may be sent and summed in bfloat16 or wider, within the bound.
A program may use at most 192 MiB of HBM per device.

v0:
```python
import jax
import jax.numpy as jnp
from jax import lax
from jax.sharding import PartitionSpec as P


def from_partner(x, axis, bit):
    return lax.ppermute(x, axis, [(i, i ^ 1 << bit) for i in range(lax.axis_size(axis))])


def prefix(x, axis, combine, identity):
    count, index = (lax.axis_size(axis), lax.axis_index(axis))
    everything = lax.all_gather(x, axis)
    start = jnp.broadcast_to(jnp.asarray(identity, x.dtype), x.shape)

    def hop(k, before):
        reached = k < index
        new = combine(before, everything[k])
        return jnp.where(reached, new, before)

    return lax.fori_loop(0, count, hop, start)


def expert_rows(inputs, w_gate, w_up, w_down):
    gate_proj = jnp.dot(inputs, w_gate, preferred_element_type=jnp.float32)
    up_proj = jnp.dot(inputs, w_up, preferred_element_type=jnp.float32)
    hidden = (jax.nn.silu(gate_proj) * up_proj).astype(jnp.bfloat16)
    return jnp.dot(hidden, w_down, preferred_element_type=jnp.float32).astype(jnp.bfloat16)


def partner_view(values):
    return from_partner(values, "rep", 0)


def pick_entry(vector, position):
    return lax.dynamic_index_in_dim(vector, position, 0, keepdims=False)


def take_rows(flat_rows, position, arrive_start, arrive_end, slot_count):
    source = jnp.sum((arrive_end[None, :] <= position[:, None]).astype(jnp.int32), axis=1)
    source = jnp.minimum(source, arrive_end.shape[0] - 1)
    offset = position - jnp.take(arrive_start, source)
    row_index = source * slot_count + offset.astype(jnp.int32)
    row_index = jnp.clip(row_index, 0, flat_rows.shape[0] - 1)
    return flat_rows[row_index]


def source_rule(queue_base, load_here, rank, hit, cap_here, cap_there, ep_index, spill_most):
    load_there = partner_view(load_here)
    spare = jnp.minimum(jnp.maximum(cap_there - load_there, 0.0), float(spill_most))
    limit_row = cap_here + spare
    kept_hit = hit * (queue_base[None, :] + rank < limit_row[None, :]).astype(jnp.float32)
    return (kept_hit, pick_entry(load_there, ep_index))


def ship_spill(
    flat_rows,
    queue_pos,
    present,
    arrive_start,
    arrive_end,
    own_load,
    cap_mine,
    cap_pair,
    load_pair,
    slot_count,
    cap_most,
    spill_most,
    weights,
):
    gate_w, up_w, down_w = weights
    zero_value = jnp.zeros((), jnp.bfloat16)
    free_here = jnp.minimum(jnp.maximum(cap_mine - own_load, 0.0), float(spill_most))
    free_there = jnp.minimum(jnp.maximum(cap_pair - load_pair, 0.0), float(spill_most))
    buffer_pos = jnp.arange(cap_most, dtype=jnp.float32)
    spill_pos = jnp.arange(spill_most, dtype=jnp.float32)
    spill_count = jnp.minimum(jnp.maximum(own_load - cap_mine, 0.0), free_there)
    spill_rows = take_rows(flat_rows, cap_mine + spill_pos, arrive_start, arrive_end, slot_count)
    outgoing = jnp.where((spill_pos < spill_count)[:, None], spill_rows, zero_value)
    incoming = from_partner(outgoing, "rep", 0)
    taken_in = jnp.minimum(jnp.maximum(load_pair - cap_pair, 0.0), free_here)
    own_rows = take_rows(flat_rows, buffer_pos, arrive_start, arrive_end, slot_count)
    in_index = jnp.clip((buffer_pos - own_load).astype(jnp.int32), 0, spill_most - 1)
    own_used = jnp.minimum(own_load, cap_mine)
    from_pair = (buffer_pos >= own_load) & (buffer_pos < own_load + taken_in)
    stacked = jnp.where(
        (buffer_pos < own_used)[:, None],
        own_rows,
        jnp.where(from_pair[:, None], incoming[in_index], zero_value),
    )
    computed = expert_rows(stacked, gate_w, up_w, down_w)
    back_index = jnp.clip((own_load + spill_pos).astype(jnp.int32), 0, cap_most - 1)
    going_back = jnp.where((spill_pos < taken_in)[:, None], computed[back_index], zero_value)
    came_back = from_partner(going_back, "rep", 0)
    queue_flat = queue_pos.reshape(-1)
    present_flat = present.reshape(-1)
    primary = present_flat & (queue_flat < cap_mine)
    spilled = present_flat & (queue_flat >= cap_mine) & (queue_flat - cap_mine < free_there)
    own_index = jnp.clip(queue_flat.astype(jnp.int32), 0, cap_most - 1)
    far_index = jnp.clip((queue_flat - cap_mine).astype(jnp.int32), 0, spill_most - 1)
    return jnp.where(
        primary[:, None],
        computed[own_index],
        jnp.where(spilled[:, None], came_back[far_index], zero_value),
    )


def on_device(tokens, routes, gate_scores, slot_order, capacity, w_gate, w_up, w_down):
    experts = lax.axis_size("ep")
    groups = lax.axis_size("rep")
    tok_rows, top_count = routes.shape
    model_width = tokens.shape[1]
    window_least = (4 * experts + 4) // 5
    slot_count = (tok_rows * top_count + window_least - 1) // window_least
    cap_most = 3 * tok_rows * top_count // 2
    spill_most = cap_most // 2
    ep_index = lax.axis_index("ep")
    rep_index = lax.axis_index("rep")
    cap_here = pick_entry(capacity, rep_index).astype(jnp.float32)
    cap_there = pick_entry(capacity, jnp.bitwise_xor(rep_index, 1) % groups).astype(jnp.float32)
    expert_ids = jnp.arange(experts, dtype=jnp.int32)
    onehot = (routes[:, :, None] == expert_ids[None, None, :]).astype(jnp.float32)
    hit = jnp.sum(onehot, axis=1)
    priority = slot_order[0]
    before = (priority[None, :] < priority[:, None]).astype(jnp.float32)
    rank = jnp.dot(before, hit, precision=lax.Precision.HIGHEST)
    counts = jnp.sum(hit, axis=0)
    slot_ids = jnp.arange(slot_count, dtype=jnp.float32)
    slot_match = hit[:, :, None] * (rank[:, :, None] == slot_ids[None, None, :]).astype(jnp.float32)
    token_ids = jnp.arange(tok_rows, dtype=jnp.float32)
    source_token = jnp.sum(slot_match * token_ids[:, None, None], axis=0).astype(jnp.int32)
    filled = slot_ids[None, :] < counts[:, None]
    outgoing = jnp.where(filled[:, :, None], tokens[source_token], jnp.zeros((), jnp.bfloat16))
    upper_part = jnp.floor(counts / 16.0)
    lower_part = counts - 16.0 * upper_part
    count_pair = jnp.stack([upper_part, lower_part], axis=1).astype(jnp.bfloat16)
    queue_base = prefix(
        counts, "ep", lambda earlier, later: earlier + later, jnp.zeros_like(counts)
    )
    load_here = lax.psum(counts, "ep")
    kept_hit, load_pair = source_rule(
        queue_base, load_here, rank, hit, cap_here, cap_there, ep_index, spill_most
    )
    arrived, arrived_pair = (
        lax.all_to_all(outgoing, "ep", split_axis=0, concat_axis=0, tiled=True),
        lax.all_to_all(count_pair, "ep", split_axis=0, concat_axis=0, tiled=True),
    )
    pair_values = arrived_pair.astype(jnp.float32)
    arrived_counts = 16.0 * pair_values[:, 0] + pair_values[:, 1]
    arrive_end = jnp.cumsum(arrived_counts)
    arrive_start = arrive_end - arrived_counts
    own_load = jnp.sum(arrived_counts)
    cap_mine = pick_entry(cap_here, ep_index)
    cap_pair = pick_entry(cap_there, ep_index)
    queue_pos = arrive_start[:, None] + slot_ids[None, :]
    present = slot_ids[None, :] < arrived_counts[:, None]
    flat_rows = arrived.reshape(experts * slot_count, model_width)
    weights = (w_gate[0], w_up[0], w_down[0])
    results = ship_spill(
        flat_rows,
        queue_pos,
        present,
        arrive_start,
        arrive_end,
        own_load,
        cap_mine,
        cap_pair,
        load_pair,
        slot_count,
        cap_most,
        spill_most,
        weights,
    )
    results = results.reshape(experts, slot_count, model_width)
    returned = lax.all_to_all(results, "ep", split_axis=0, concat_axis=0, tiled=True)
    kept_mask = jnp.sum(onehot * kept_hit[:, None, :], axis=2)
    rank_pick = jnp.sum(onehot * rank[:, None, :], axis=2).astype(jnp.int32)
    row_index = routes * slot_count + rank_pick
    picked = returned.reshape(experts * slot_count, model_width)[row_index]
    gate_total = jnp.sum(gate_scores, axis=1)
    kept_sum = jnp.sum(gate_scores * kept_mask, axis=1)
    weight = gate_scores * kept_mask / jnp.maximum(kept_sum, 0.25 * gate_total)[:, None]
    mixed = jnp.sum(weight[:, :, None] * picked.astype(jnp.float32), axis=1)
    return mixed.astype(jnp.bfloat16)


def solution(mesh):
    placed = (
        P(("rep", "ep"), None),
        P(("rep", "ep"), None),
        P(("rep", "ep"), None),
        P(("rep", "ep"), None),
        P(),
        P("ep", None, None),
        P("ep", None, None),
        P("ep", None, None),
    )
    return jax.shard_map(
        on_device, mesh=mesh, in_specs=placed, out_specs=P(("rep", "ep"), None), check_vma=False
    )
```

profile of v0, /device:TPU:0, one launch (start us, length us, event | category | flops | bytes accessed | tf_op | source)
XLA Modules:
  0.0 848.7 jit_solution(13659958271864282128)
XLA Ops:
  0.0 0.9 convert_reduce_fusion.2
  0.9 1.2 dynamic-slice.2
  2.8 0.2 dynamic-update-slice
  3.1 69.4 %all-reduce.1 = (f32[32]{0:T(128)S(1)}, f32[1024]{0:T(1024)S(1)}) all-reduce(f32[32]{0:T(128)S(1)} %get-tuple-element.127, f32[1024]{0:T(1024)S(1)} %dynamic-update-slice), channel_id=1, replica_groups=mesh['rep'=4,'ep'=32] {'ep'}, use_global_device_ids=true, to_apply=%region_4.5 | all-reduce | flops 1056 | bytes 8448 | tf_op jit(solution)/shard_map/psum | solution.py:140
  72.5 1.7 collective-permute-start
  74.2 0.7 copy.52
  74.9 3.8 all-to-all-start
  78.9 1.3 while.14
  80.2 0.8 fusion.36
  81.0 1.6 fusion.18
  82.6 0.2 multiply_reduce_fusion
  82.8 0.3 copy-done.4
  83.3 8.2 gather_fusion
  91.5 9.9 %broadcast_select_fusion.2 = bf16[32,40,4096]{2,1,0:T(8,128)(2,1)} fusion(bf16[32,40,4096]{2,1,0:T(8,128)(2,1)} %bitcast.98, pred[32,40]{1,0:T(8,128)(4,1)S(1)} %iota_compare_fusion.3), kind=kLoop, calls=%fused_computation.15 | loop fusion | flops 5242880 | bytes 20972800 | tf_op jit(solution)/shard_map/jit(_where)/select_n | solution.py:133
  101.4 7.5 all-to-all-start.1
  109.0 0.1 copy.53
  109.0 0.7 fusion.41
  109.9 0.6 copy-done.2
  110.5 0.1 reduce.2
  110.6 0.7 fusion.43
  111.3 0.7 fusion.42
  112.0 0.6 constant_dynamic-slice_fusion
  113.8 0.7 dynamic_slice.29
  115.8 0.6 iota_add_fusion.1
  116.4 0.1 convert_reduce_fusion.3
  116.5 4.3 fusion.26
  120.7 0.2 compare_reduce_fusion.49
  120.9 15.3 %select_select_fusion.3 = f32[768]{0:T(1024)S(1)} fusion(pred[768]{0:T(1024)(128)(4,1)S(1)} %get-tuple-element.152, pred[768]{0:T(1024)(128)(4,1)S(1)} %get-tuple-element.151, pred[768]{0:T(1024)(128)(4,1)S(1)} %get-tuple-element.153, pred[768]{0:T(1024)(128)(4,1)S(1)} %get-tuple-element.150, pred[768]{0:T(1024)(128)(4,1)S(1)} %get-tuple-element.149, ...), kind=kLoop, calls=%fused_computation.145 | loop fusion | flops 19200 | bytes 25444 | tf_op jit(solution)/shard_map/jit(_take)/gather | solution.py:42
  136.3 0.6 fusion.27
  136.9 105.5 %all-to-all-done.1 = bf16[32,40,4096]{2,1,0:T(8,128)(2,1)} async-done(((bf16[32,40,4096]{2,1,0:T(8,128)(2,1)}), bf16[32,40,4096]{2,1,0:T(8,128)(2,1)}, u32[]{:S(2)}, u32[]{:S(2)}) %all-to-all-start.1) | async-done | bytes 10485792 | tf_op jit(solution)/shard_map/all_to_all | solution.py:145
  242.3 17.3 %gather_fusion.2 = bf16[768,4096]{1,0:T(8,128)(2,1)} fusion(bf16[1280,4096]{1,0:T(8,128)(2,1)} %bitcast.14, s32[1024]{0:T(1024)S(1)} %pad_clamp_fusion.6), kind=kCustom, calls=%fused_computation.2 | custom fusion | bytes 12585984 | tf_op jit(solution)/shard_map/gather | solution.py:45
  259.7 6.0 broadcast_select_fusion.4
  265.6 0.6 collective-permute-start.1
  266.3 0.7 fusion.28
  267.0 0.7 fusion.22
  267.7 0.1 convert_reduce_fusion
  267.8 4.3 fusion.20
  272.1 0.4 compare_reduce_fusion.24
  272.6 15.3 %select_select_fusion.2 = f32[1536]{0:T(1024)S(1)} fusion(pred[1536]{0:T(1024)(128)(4,1)S(1)} %get-tuple-element.123, pred[1536]{0:T(1024)(128)(4,1)S(1)} %get-tuple-element.122, pred[1536]{0:T(1024)(128)(4,1)S(1)} %get-tuple-element.124, pred[1536]{0:T(1024)(128)(4,1)S(1)} %get-tuple-element.121, pred[1536]{0:T(1024)(128)(4,1)S(1)} %get-tuple-element.120, ...), kind=kLoop, calls=%fused_computation.132 | loop fusion | flops 38400 | bytes 50788 | tf_op jit(solution)/shard_map/jit(_take)/gather | solution.py:42
  292.4 0.7 fusion.19
  293.1 27.4 %gather_fusion.1 = bf16[1536,4096]{1,0:T(8,128)(2,1)} fusion(bf16[1280,4096]{1,0:T(8,128)(2,1)} %bitcast.14, s32[2048]{0:T(1024)S(1)} %pad_clamp_fusion.3), kind=kCustom, calls=%fused_computation.1 | custom fusion | bytes 25171968 | tf_op jit(solution)/shard_map/gather | solution.py:45
  320.5 75.7 %collective-permute-done.1 = bf16[768,4096]{1,0:T(8,128)(2,1)} collective-permute-done((bf16[768,4096]{1,0:T(8,128)(2,1)}, bf16[768,4096]{1,0:T(8,128)(2,1)}, u32[]{:S(2)}, u32[]{:S(2)}) %collective-permute-start.1) | collective-permute-done | bytes 6291488 | tf_op jit(solution)/shard_map/ppermute | solution.py:8
  396.2 25.7 %gather_fusion.3 = bf16[1536,4096]{1,0:T(8,128)(2,1)} fusion(bf16[768,4096]{1,0:T(8,128)(2,1)} %collective-permute-done.1, s32[2048]{0:T(1024)S(1)} %pad_clamp_fusion.2), kind=kCustom, calls=%fused_computation.3 | custom fusion | bytes 25171968 | tf_op jit(solution)/shard_map/gather | solution.py:89
  421.9 19.5 %fusion.2 = f32[1536,768]{1,0:T(8,128)} fusion(bf16[1,4096,768]{2,1,0:T(8,128)(2,1)} %param.16, bf16[1536,4096]{1,0:T(8,128)(2,1)} %gather_fusion.1, bf16[1536,4096]{1,0:T(8,128)(2,1)} %gather_fusion.3, pred[1536]{0:T(1024)(128)(4,1)S(1)} %fusion.19, pred[1536]{0:T(1024)(128)(4,1)S(1)} %iota_compare_fusion.7), kind=kOutput, calls=%fused_computation.17 | convolution fusion | flops 9676259328 | bytes 36178944 | tf_op jit(solution)/shard_map/dot_general | solution.py:26
  441.4 19.0 %fusion.4 = f32[1536,768]{1,0:T(8,128)} fusion(bf16[1,4096,768]{2,1,0:T(8,128)(2,1)} %param.15, bf16[1536,4096]{1,0:T(8,128)(2,1)} %gather_fusion.1, bf16[1536,4096]{1,0:T(8,128)(2,1)} %gather_fusion.3, pred[1536]{0:T(1024)(128)(4,1)S(1)} %fusion.19, pred[1536]{0:T(1024)(128)(4,1)S(1)} %iota_compare_fusion.7), kind=kOutput, calls=%fused_computation.19 | convolution fusion | flops 9676259328 | bytes 36178944 | tf_op jit(solution)/shard_map/dot_general | solution.py:25
  460.4 16.8 %convolution_convert_fusion = bf16[1536,4096]{1,0:T(8,128)(2,1)} fusion(bf16[1,768,4096]{2,1,0:T(8,128)(2,1)S(1)} %bitcast.101, f32[1536,768]{1,0:T(8,128)} %fusion.2, f32[1536,768]{1,0:T(8,128)} %fusion.4), kind=kOutput, calls=%fused_computation.12 | convolution fusion | flops 9677045760 | bytes 28311552 | tf_op jit(solution)/shard_map/dot_general | solution.py:28
  477.2 18.1 %gather_fusion.5 = bf16[768,4096]{1,0:T(8,128)(2,1)} fusion(bf16[1536,4096]{1,0:T(8,128)(2,1)} %convolution_convert_fusion, s32[1024]{0:T(1024)S(1)} %pad_clamp_fusion.5), kind=kCustom, calls=%fused_computation.5 | custom fusion | bytes 12585984 | tf_op jit(solution)/shard_map/gather | solution.py:93
  495.4 5.9 broadcast_select_fusion.3
  501.3 0.5 collective-permute-start.2
  501.8 0.6 convert_clamp_fusion
  502.5 0.1 min.144
  502.6 0.1 min.149
  502.7 0.6 fusion.16
  503.4 25.1 %gather_fusion.4 = bf16[1280,4096]{1,0:T(8,128)(2,1)} fusion(bf16[1536,4096]{1,0:T(8,128)(2,1)} %convolution_convert_fusion, s32[2048]{0:T(1024)S(1)} %pad_clamp_fusion.1), kind=kCustom, calls=%fused_computation.4 | custom fusion | bytes 20976640 | tf_op jit(solution)/shard_map/gather | solution.py:103
  528.5 102.3 %collective-permute-done.2 = bf16[768,4096]{1,0:T(8,128)(2,1)} collective-permute-done((bf16[768,4096]{1,0:T(8,128)(2,1)}, bf16[768,4096]{1,0:T(8,128)(2,1)}, u32[]{:S(2)}, u32[]{:S(2)}) %collective-permute-start.2) | collective-permute-done | bytes 6291488 | tf_op jit(solution)/shard_map/ppermute | solution.py:8
  630.8 22.3 %gather_fusion.6 = bf16[1280,4096]{1,0:T(8,128)(2,1)} fusion(bf16[768,4096]{1,0:T(8,128)(2,1)} %collective-permute-done.2, s32[2048]{0:T(1024)S(1)} %pad_clamp_fusion), kind=kCustom, calls=%fused_computation.6 | custom fusion | bytes 20976640 | tf_op jit(solution)/shard_map/gather | solution.py:104
  653.1 12.2 %select_select_fusion.1 = bf16[32,40,4096]{2,1,0:T(8,128)(2,1)} fusion(bf16[32,40,4096]{2,1,0:T(8,128)(2,1)} %bitcast.96, bf16[32,40,4096]{2,1,0:T(8,128)(2,1)} %bitcast.97, pred[32,40]{1,0:T(8,128)(4,1)S(1)} %get-tuple-element.177, pred[32,40]{1,0:T(8,128)(4,1)S(1)} %get-tuple-element.176), kind=kLoop, calls=%fused_computation.14 | loop fusion | flops 10485760 | bytes 31459840 | tf_op jit(solution)/shard_map/jit(_where)/select_n | solution.py:101
  665.4 16.1 %all-to-all-start.2 = ((bf16[32,40,4096]{2,1,0:T(8,128)(2,1)}), bf16[32,40,4096]{2,1,0:T(8,128)(2,1)}, u32[]{:S(2)}, u32[]{:S(2)}) async-start(bf16[32,40,4096]{2,1,0:T(8,128)(2,1)} %select_select_fusion.1), calls=%async_computation.2 | async-start | bytes 20971520 | tf_op jit(solution)/shard_map/all_to_all | solution.py:175
  681.6 0.1 copy.56
  681.7 0.1 reshape.596
  681.8 0.1 copy.51
  681.9 132.9 %all-to-all-done.2 = bf16[32,40,4096]{2,1,0:T(8,128)(2,1)} async-done(((bf16[32,40,4096]{2,1,0:T(8,128)(2,1)}), bf16[32,40,4096]{2,1,0:T(8,128)(2,1)}, u32[]{:S(2)}, u32[]{:S(2)}) %all-to-all-start.2) | async-done | bytes 10485792 | tf_op jit(solution)/shard_map/all_to_all | solution.py:175
  814.8 20.5 %gather_fusion.7 = bf16[1024,4096]{1,0:T(8,128)(2,1)} fusion(bf16[1280,4096]{1,0:T(8,128)(2,1)} %bitcast.55, s32[1024]{0:T(1024)S(1)} %broadcast_clamp_fusion), kind=kCustom, calls=%fused_computation.7 | custom fusion | bytes 16781312 | tf_op jit(solution)/shard_map/gather | solution.py:179
  835.3 12.9 %fusion = bf16[128,4096]{1,0:T(8,128)(2,1)} fusion(bf16[1024,4096]{1,0:T(8,128)(2,1)} %gather_fusion.7, f32[128,8]{1,0:T(8,128)S(1)} %copy.51), kind=kLoop, calls=%fused_computation.11 | loop fusion | flops 12058624 | bytes 9441280 | tf_op jit(solution)/shard_map/reduce_sum | solution.py:183
  (94 shorter events, 1.4 us)
Async XLA Ops:
  0.0 83.3 %copy-start = (bf16[128,4096]{1,0:T(8,128)(2,1)S(1)}, bf16[128,4096]{1,0:T(8,128)(2,1)}, u32[]{:S(2)}) copy-start(bf16[128,4096]{1,0:T(8,128)(2,1)} %param.10) | copy-start | bytes 3145732
  72.5 7.7 collective-permute-start
  74.9 26.5 %all-to-all-start = ((bf16[32,1,2]{2,1,0:T(2,128)(2,1)}), bf16[32,1,2]{2,1,0:T(2,128)(2,1)S(1)}, u32[]{:S(2)}, u32[]{:S(2)}) async-start(bf16[32,1,2]{2,1,0:T(2,128)(2,1)} %copy.52), calls=%async_computation | async-start | bytes 32768 | tf_op jit(solution)/shard_map/all_to_all | solution.py:146
  82.6 0.6 copy-start.4
  101.4 140.9 %all-to-all-start.1 = ((bf16[32,40,4096]{2,1,0:T(8,128)(2,1)}), bf16[32,40,4096]{2,1,0:T(8,128)(2,1)}, u32[]{:S(2)}, u32[]{:S(2)}) async-start(bf16[32,40,4096]{2,1,0:T(8,128)(2,1)} %broadcast_select_fusion.2), calls=%async_computation.1 | async-start | bytes 20971520 | tf_op jit(solution)/shard_map/all_to_all | solution.py:145
  109.7 150.0 %copy-start.8 = (f32[32,1]{0,1:T(1,128)}, f32[32,1]{0,1:T(1,128)S(1)}, u32[]{:S(2)}) copy-start(f32[32,1]{0,1:T(1,128)S(1)} %get-tuple-element.170) | copy-start | bytes 388
  109.9 0.6 copy-start.2
  265.6 130.6 %collective-permute-start.1 = (bf16[768,4096]{1,0:T(8,128)(2,1)}, bf16[768,4096]{1,0:T(8,128)(2,1)}, u32[]{:S(2)}, u32[]{:S(2)}) collective-permute-start(bf16[768,4096]{1,0:T(8,128)(2,1)} %broadcast_select_fusion.4), channel_id=1, source_target_pairs={{0,32},{32,0},{64,96},{96,64},{1,33},{33,1},{65,97},{97,65},{2,34}... | collective-permute-start | bytes 18874376 | tf_op jit(solution)/shard_map/ppermute | solution.py:8
  421.9 38.5 %slice-start = ((s8[6291456]{0:T(1024)(128)(4,1)}), s8[4194304]{0:T(1024)(128)(4,1)S(1)}, s32[]{:S(2)}) async-start(s8[6291456]{0:T(1024)(128)(4,1)} %bitcast.100), calls=%async_computation.3 | async-start | bytes 8388608
  441.4 19.0 %slice-start.1 = ((s8[6291456]{0:T(1024)(128)(4,1)}), s8[2097152]{0:T(1024)(128)(4,1)S(1)}, s32[]{:S(2)}) async-start(s8[6291456]{0:T(1024)(128)(4,1)} %bitcast.100), calls=%async_computation.4 | async-start | bytes 4194304
  495.4 6.4 copy-start.3
  495.4 6.5 copy-start.9
  501.3 129.5 %collective-permute-start.2 = (bf16[768,4096]{1,0:T(8,128)(2,1)}, bf16[768,4096]{1,0:T(8,128)(2,1)}, u32[]{:S(2)}, u32[]{:S(2)}) collective-permute-start(bf16[768,4096]{1,0:T(8,128)(2,1)} %broadcast_select_fusion.3), channel_id=1, source_target_pairs={{0,32},{32,0},{64,96},{96,64},{1,33},{33,1},{65,97},{97,65},{2,34}... | collective-permute-start | bytes 18874376 | tf_op jit(solution)/shard_map/ppermute | solution.py:8
  665.3 16.1 %copy-start.5 = (f32[128,32]{0,1:T(8,128)S(1)}, f32[128,32]{0,1:T(8,128)}, u32[]{:S(2)}) copy-start(f32[128,32]{0,1:T(8,128)} %copy-done.4) | copy-start | bytes 49156
  665.3 16.1 %copy-start.6 = (s32[128,8]{0,1:T(8,128)S(1)}, s32[128,8]{0,1:T(8,128)}, u32[]{:S(2)}) copy-start(s32[128,8]{0,1:T(8,128)} %param.11) | copy-start | bytes 12292
  665.3 16.1 %copy-start.7 = (f32[128,32]{0,1:T(8,128)S(1)}, f32[128,32]{0,1:T(8,128)}, u32[]{:S(2)}) copy-start(f32[128,32]{0,1:T(8,128)} %get-tuple-element.214) | copy-start | bytes 49156
  665.3 16.4 %copy-start.10 = (f32[128,8]{0,1:T(8,128)S(1)}, f32[128,8]{0,1:T(8,128)}, u32[]{:S(2)}) copy-start(f32[128,8]{0,1:T(8,128)} %param.12) | copy-start | bytes 12292
  665.4 149.5 %all-to-all-start.2 = ((bf16[32,40,4096]{2,1,0:T(8,128)(2,1)}), bf16[32,40,4096]{2,1,0:T(8,128)(2,1)}, u32[]{:S(2)}, u32[]{:S(2)}) async-start(bf16[32,40,4096]{2,1,0:T(8,128)(2,1)} %select_select_fusion.1), calls=%async_computation.2 | async-start | bytes 20971520 | tf_op jit(solution)/shard_map/all_to_all | solution.py:175
  814.8 33.4 %copy-start.1 = (bf16[128,4096]{1,0:T(8,128)(2,1)S(1)}, bf16[128,4096]{1,0:T(8,128)(2,1)}, u32[]{:S(2)}) copy-start(bf16[128,4096]{1,0:T(8,128)(2,1)} %param.10) | copy-start | bytes 3145732
where the time goes:
time: 858 us; the launch traced here: 849 us
  waiting for transfers between devices  416 us (48%)
  local copies, waits for them, and re-layouts  171 us (20%)
  other arithmetic  95.2 us (11%)
  blocking collectives  69.4 us (8%)
  matrix products  56.9 us (7%)
  starting transfers between devices  30.1 us (4%)
    ppermute x3, waiting for transfers between devices, from_partner(): lax.ppermute(x, axis, [(i, i ^ 1 << bit) for i in range(lax.axis_size(axi...  178 us
    all_to_all x1, waiting for transfers between devices, on_device(): lax.all_to_all(results, 'ep', split_axis=0, concat_axis=0, tiled=True)  133 us
    all_to_all x1, waiting for transfers between devices, on_device(): lax.all_to_all(outgoing, 'ep', split_axis=0, concat_axis=0, tiled=True)  105 us
    psum x1, blocking collectives, on_device(): load_here = lax.psum(counts, 'ep')  69.4 us
    gather x2, local copies, waits for them, and re-layouts, take_rows(): return flat_rows[row_index]  44.7 us
    gather x6, other arithmetic, take_rows(): offset = position - jnp.take(arrive_start, source)  39.9 us
    gather x1, local copies, waits for them, and re-layouts, ship_spill(): incoming[in_index]  25.7 us
    gather x1, local copies, waits for them, and re-layouts, ship_spill(): computed[own_index]  25.1 us
  transfers between devices with their start and end apart: 6, of which 4 were waited for; matrix products, arithmetic and copies ran while one was open for 15% of the time, Pallas kernels for 0%

commit v1 on v0

v1 whole, which is shorter than its diff:
```python
import jax
import jax.numpy as jnp
from jax import lax
from jax.sharding import PartitionSpec as P

SLOT = 40
SPILL = 768.0


def routing(routes, slot_order, capacity):
    experts = lax.axis_size("ep")
    groups = lax.axis_size("rep")
    ep_index = lax.axis_index("ep")
    rep_index = lax.axis_index("rep")
    expert_ids = jnp.arange(experts, dtype=jnp.int32)
    onehot = (routes[:, :, None] == expert_ids[None, None, :]).astype(jnp.float32)
    hit = jnp.sum(onehot, axis=1)
    priority = slot_order[0]
    before = (priority[None, :] < priority[:, None]).astype(jnp.float32)
    rank = jnp.dot(before, hit, precision=lax.Precision.HIGHEST)
    counts = jnp.sum(hit, axis=0)
    every = lax.all_gather(counts, ("rep", "ep")).reshape(groups, experts, experts)
    here = lax.dynamic_index_in_dim(every, rep_index, 0, keepdims=False)
    pair = jnp.bitwise_xor(rep_index, 1) % groups
    there = lax.dynamic_index_in_dim(every, pair, 0, keepdims=False)
    earlier = (jnp.arange(experts) < ep_index).astype(jnp.float32)
    start = jnp.sum(here * earlier[:, None], axis=0)
    load_there = jnp.sum(there, axis=0)
    caps = capacity.astype(jnp.float32)
    cap_here = lax.dynamic_index_in_dim(caps, rep_index, 0, keepdims=False)
    cap_there = lax.dynamic_index_in_dim(caps, pair, 0, keepdims=False)
    limit = cap_here + jnp.minimum(jnp.maximum(cap_there - load_there, 0.0), SPILL)
    kept_hit = hit * (start[None, :] + rank < limit[None, :]).astype(jnp.float32)
    return onehot, hit, rank, counts, kept_hit


def expert_rows(inputs, w_gate, w_up, w_down):
    gate_proj = jnp.dot(inputs, w_gate, preferred_element_type=jnp.float32)
    up_proj = jnp.dot(inputs, w_up, preferred_element_type=jnp.float32)
    hidden = (jax.nn.silu(gate_proj) * up_proj).astype(jnp.bfloat16)
    return jnp.dot(hidden, w_down, preferred_element_type=jnp.float32).astype(jnp.bfloat16)


def on_device(tokens, routes, gate_scores, slot_order, capacity, w_gate, w_up, w_down):
    experts = lax.axis_size("ep")
    tok_rows, width = tokens.shape
    onehot, hit, rank, counts, kept_hit = routing(routes, slot_order, capacity)
    slot_ids = jnp.arange(SLOT, dtype=jnp.float32)
    slot_match = hit[:, :, None] * (rank[:, :, None] == slot_ids[None, None, :]).astype(jnp.float32)
    token_ids = jnp.arange(tok_rows, dtype=jnp.float32)
    select = slot_match.reshape(tok_rows, experts * SLOT).astype(jnp.bfloat16)
    outgoing = lax.dot_general(
        select, tokens, (((0,), (0,)), ((), ())), preferred_element_type=jnp.float32
    ).astype(jnp.bfloat16)
    outgoing = outgoing.reshape(experts, SLOT, width)
    arrived = lax.all_to_all(outgoing, "ep", split_axis=0, concat_axis=0, tiled=True)
    results = expert_rows(arrived.reshape(experts * SLOT, width), w_gate[0], w_up[0], w_down[0])
    returned = lax.all_to_all(
        results.reshape(experts, SLOT, width), "ep", split_axis=0, concat_axis=0, tiled=True
    )
    kept_mask = jnp.sum(onehot * kept_hit[:, None, :], axis=2)
    rank_pick = jnp.sum(onehot * rank[:, None, :], axis=2).astype(jnp.int32)
    row_index = routes * SLOT + rank_pick
    picked = returned.reshape(experts * SLOT, width)[row_index]
    gate_total = jnp.sum(gate_scores, axis=1)
    kept_sum = jnp.sum(gate_scores * kept_mask, axis=1)
    weight = gate_scores * kept_mask / jnp.maximum(kept_sum, 0.25 * gate_total)[:, None]
    mixed = jnp.sum(weight[:, :, None] * picked.astype(jnp.float32), axis=1)
    return mixed.astype(jnp.bfloat16)


def solution(mesh):
    placed = (
        P(("rep", "ep"), None),
        P(("rep", "ep"), None),
        P(("rep", "ep"), None),
        P(("rep", "ep"), None),
        P(),
        P("ep", None, None),
        P("ep", None, None),
        P("ep", None, None),
    )
    return jax.shard_map(
        on_device, mesh=mesh, in_specs=placed, out_specs=P(("rep", "ep"), None), check_vma=False
    )
```

time: 858 us -> 405 us (0.47)
  waiting for transfers between devices: 416 us -> 133 us
  local copies, waits for them, and re-layouts: 171 us -> 21.3 us
  blocking collectives: 69.4 us -> 191 us
  other arithmetic: 95.2 us -> 15 us
  starting transfers between devices: 30.1 us -> 5.12 us
  matrix products: 56.9 us -> 38.9 us
    ppermute x3 -> x0, waiting for transfers between devices: 178 us -> none  [from_partner(): lax.ppermute(x, axis, [(i, i ^ 1 << bit) for i in range(lax.axis_size(axi...]
    gather x10 -> x1, local copies, waits for them, and re-layouts: 166 us -> 20.5 us  [on_device(): picked = returned.reshape(experts * SLOT, width)[row_index]]
    all_to_all x0 -> x1, blocking collectives: none -> 122 us  [on_device(): lax.all_to_all(outgoing, 'ep', split_axis=0, concat_axis=0, tiled=True)]
    all_to_all x3 -> x1, waiting for transfers between devices: 238 us -> 133 us  [on_device(): lax.all_to_all(results.reshape(experts, SLOT, width), 'ep', split_axis=0,...]
    psum x1 -> x0, blocking collectives: 69.4 us -> none  [on_device(): load_here = lax.psum(counts, 'ep')]
    unnamed x0 -> x1, blocking collectives: none -> 68.2 us
    gather x14 -> x1, other arithmetic: 39.9 us -> 0.01 us  [on_device(): picked = returned.reshape(experts * SLOT, width)[row_index]]
    select_n x44 -> x1, other arithmetic: 36.7 us -> 0.01 us  [on_device(): picked = returned.reshape(experts * SLOT, width)[row_index]]
  transfers between devices with their start and end apart: 6 -> 1, of which waited for: 4 -> 1; matrix products, arithmetic and copies ran while one was open for 15% -> 0% of each run, Pallas kernels for 0% -> 0%
where the time goes in v1:
time: 405 us; the launch traced here: 404 us
  blocking collectives  191 us (47%)
  waiting for transfers between devices  133 us (33%)
  matrix products  38.9 us (10%)
  local copies, waits for them, and re-layouts  21.3 us (5%)
  other arithmetic  15 us (4%)
  starting transfers between devices  5.12 us (1%)
    all_to_all x1, waiting for transfers between devices, on_device(): lax.all_to_all(results.reshape(experts, SLOT, width), 'ep', split_axis=0,...  133 us
    all_to_all x1, blocking collectives, on_device(): lax.all_to_all(outgoing, 'ep', split_axis=0, concat_axis=0, tiled=True)  122 us
    unnamed x1, blocking collectives  68.2 us
    gather x1, local copies, waits for them, and re-layouts, on_device(): picked = returned.reshape(experts * SLOT, width)[row_index]  20.5 us
    dot_general x1, matrix products, expert_rows(): jnp.dot(hidden, w_down, preferred_element_type=jnp.float32)  13.4 us
    reduce_sum x1, other arithmetic, on_device(): mixed = jnp.sum(weight[:, :, None] * picked.astype(jnp.float32), axis=1)  12.9 us
    dot_general x1, matrix products, expert_rows(): gate_proj = jnp.dot(inputs, w_gate, preferred_element_type=jnp.float32)  12.4 us
    dot_general x1, matrix products, expert_rows(): up_proj = jnp.dot(inputs, w_up, preferred_element_type=jnp.float32)  8.98 us
  transfers between devices with their start and end apart: 1, of which 1 were waited for; matrix products, arithmetic and copies ran while one was open for 0% of the time, Pallas kernels for 0%

profile of v1, /device:TPU:0, one launch (start us, length us, event | category | flops | bytes accessed | tf_op | source)
XLA Modules:
  0.0 404.1 jit_solution(6809308742256987934)
XLA Ops:
  0.0 0.0 copy-start
  0.0 0.9 convert_reduce_fusion.1
  0.9 0.3 dynamic-update-slice
  1.2 68.2 %all-reduce = f32[4096]{0:T(1024)S(1)} all-reduce(f32[4096]{0:T(1024)S(1)} %dynamic-update-slice), channel_id=2, replica_groups=mesh['rep'=4,'ep'=32] {'rep','ep'}, use_global_device_ids=true, to_apply=%add | all-reduce | flops 4096 | bytes 32768
  69.4 0.1 reshape.39
  69.5 0.7 convert_element_type.39
  70.2 0.1 eq.41
  70.3 0.1 fusion.17
  70.4 1.0 fusion.18
  71.4 0.3 fusion.12
  71.7 0.0 copy-done
  71.7 3.1 convolution_convert_fusion.1
  74.7 0.0 slice-start
  74.7 122.5 %all_to_all.10 = bf16[32,40,4096]{2,1,0:T(8,128)(2,1)S(1)} all-to-all(bf16[32,40,4096]{2,1,0:T(8,128)(2,1)S(1)} %bitcast.43), channel_id=1, replica_groups=mesh['rep'=4,'ep'=32] {'ep'}, dimensions={0} | all-to-all | bytes 20971520 | tf_op jit(solution)/shard_map/all_to_all | solution.py:56
  197.2 0.0 slice-start.1
  197.2 12.4 %fusion.4 = f32[1280,768]{1,0:T(8,128)S(1)} fusion(bf16[1280,4096]{1,0:T(8,128)(2,1)S(1)} %bitcast.45, bf16[1,4096,768]{2,1,0:T(8,128)(2,1)} %param.13), kind=kOutput, calls=%fused_computation.8 | convolution fusion | flops 8053063680 | bytes 20709376 | tf_op jit(solution)/shard_map/dot_general | solution.py:38
  209.7 0.0 slice-done
  209.7 0.0 slice-done.1
  209.7 9.0 %fusion.9 = bf16[1280,768]{1,0:T(8,128)(2,1)S(1)} fusion(bf16[1280,4096]{1,0:T(8,128)(2,1)S(1)} %bitcast.46, bf16[1,4096,768]{2,1,0:T(8,128)(2,1)S(1)} %bitcast.48, f32[1280,768]{1,0:T(8,128)S(1)} %fusion.4), kind=kOutput, calls=%fused_computation.11 | convolution fusion | flops 8058961920 | bytes 22675456 | tf_op jit(solution)/shard_map/dot_general | solution.py:39
  218.7 13.4 %convolution_convert_fusion = bf16[1280,4096]{1,0:T(8,128)(2,1)} fusion(bf16[1280,768]{1,0:T(8,128)(2,1)S(1)} %fusion.9, bf16[1,768,4096]{2,1,0:T(8,128)(2,1)} %param.15), kind=kOutput, calls=%fused_computation.3 | convolution fusion | flops 8058306560 | bytes 18743296 | tf_op jit(solution)/shard_map/dot_general | solution.py:41
  232.1 0.0 copy-start.2
  232.1 0.0 copy-start.3
  232.2 5.1 %all-to-all-start.1 = ((bf16[32,40,4096]{2,1,0:T(8,128)(2,1)}), bf16[32,40,4096]{2,1,0:T(8,128)(2,1)}, u32[]{:S(2)}, u32[]{:S(2)}) async-start(bf16[32,40,4096]{2,1,0:T(8,128)(2,1)} %bitcast.44), calls=%async_computation.1 | async-start | bytes 20971520 | tf_op jit(solution)/shard_map/all_to_all | solution.py:58
  237.3 0.0 copy-done.2
  237.4 0.1 copy.21
  237.5 0.1 reshape.46
  237.5 0.0 copy-done.3
  237.6 0.1 copy.20
  237.7 133.0 %all-to-all-done.1 = bf16[32,40,4096]{2,1,0:T(8,128)(2,1)} async-done(((bf16[32,40,4096]{2,1,0:T(8,128)(2,1)}), bf16[32,40,4096]{2,1,0:T(8,128)(2,1)}, u32[]{:S(2)}, u32[]{:S(2)}) %all-to-all-start.1) | async-done | bytes 10485792 | tf_op jit(solution)/shard_map/all_to_all | solution.py:58
  370.7 0.0 copy-start.1
  370.7 20.5 %gather_fusion = bf16[1024,4096]{1,0:T(8,128)(2,1)} fusion(bf16[1280,4096]{1,0:T(8,128)(2,1)} %bitcast.12, s32[1024]{0:T(1024)S(1)} %broadcast_clamp_fusion), kind=kCustom, calls=%fused_computation | custom fusion | bytes 16781312 | tf_op jit(solution)/shard_map/gather | solution.py:64
  391.2 12.9 %fusion = bf16[128,4096]{1,0:T(8,128)(2,1)} fusion(bf16[1024,4096]{1,0:T(8,128)(2,1)} %gather_fusion, f32[128,8]{1,0:T(8,128)S(1)} %copy.20), kind=kLoop, calls=%fused_computation.2 | loop fusion | flops 12058624 | bytes 9441280 | tf_op jit(solution)/shard_map/reduce_sum | solution.py:68
  404.1 0.0 copy-done.1
  (12 shorter events, 0.1 us)
Async XLA Ops:
  0.0 71.7 %copy-start = (bf16[128,4096]{1,0:T(8,128)(2,1)S(1)}, bf16[128,4096]{1,0:T(8,128)(2,1)}, u32[]{:S(2)}) copy-start(bf16[128,4096]{1,0:T(8,128)(2,1)} %param.8) | copy-start | bytes 3145732
  74.7 135.0 %slice-start = ((s8[6291456]{0:T(1024)(128)(4,1)}), s8[2097152]{0:T(1024)(128)(4,1)S(1)}, s32[]{:S(2)}) async-start(s8[6291456]{0:T(1024)(128)(4,1)} %bitcast.47), calls=%async_computation.2 | async-start | bytes 4194304
  197.2 12.5 %slice-start.1 = ((s8[6291456]{0:T(1024)(128)(4,1)}), s8[4194304]{0:T(1024)(128)(4,1)S(1)}, s32[]{:S(2)}) async-start(s8[6291456]{0:T(1024)(128)(4,1)} %bitcast.47), calls=%async_computation.3 | async-start | bytes 8388608
  232.1 5.1 %copy-start.2 = (s32[128,8]{0,1:T(8,128)S(1)}, s32[128,8]{0,1:T(8,128)}, u32[]{:S(2)}) copy-start(s32[128,8]{0,1:T(8,128)} %param.9) | copy-start | bytes 12292
  232.1 5.4 %copy-start.3 = (f32[128,8]{0,1:T(8,128)S(1)}, f32[128,8]{0,1:T(8,128)}, u32[]{:S(2)}) copy-start(f32[128,8]{0,1:T(8,128)} %param.10) | copy-start | bytes 12292
  232.2 138.5 %all-to-all-start.1 = ((bf16[32,40,4096]{2,1,0:T(8,128)(2,1)}), bf16[32,40,4096]{2,1,0:T(8,128)(2,1)}, u32[]{:S(2)}, u32[]{:S(2)}) async-start(bf16[32,40,4096]{2,1,0:T(8,128)(2,1)} %bitcast.44), calls=%async_computation.1 | async-start | bytes 20971520 | tf_op jit(solution)/shard_map/all_to_all | solution.py:58
  370.7 33.4 %copy-start.1 = (bf16[128,4096]{1,0:T(8,128)(2,1)S(1)}, bf16[128,4096]{1,0:T(8,128)(2,1)}, u32[]{:S(2)}) copy-start(bf16[128,4096]{1,0:T(8,128)(2,1)} %param.8) | copy-start | bytes 3145732

commit v2 on v1

v2 whole, which is shorter than its diff:
```python
import functools

import jax
import jax.numpy as jnp
from jax import lax
from jax.experimental import pallas as pl
from jax.experimental.pallas import tpu as pltpu
from jax.sharding import PartitionSpec as P

SPILL = 768.0
SIDE = 4
CHUNKS = 2
MESH = pl.DeviceIdType.MESH


def routing_weights(routes, gate_scores, slot_order, capacity):
    experts = lax.axis_size("ep")
    groups = lax.axis_size("rep")
    ep_index = lax.axis_index("ep")
    rep_index = lax.axis_index("rep")
    expert_ids = jnp.arange(experts, dtype=jnp.int32)
    onehot = (routes[:, :, None] == expert_ids[None, None, :]).astype(jnp.float32)
    hit = jnp.sum(onehot, axis=1)
    score = jnp.sum(onehot * gate_scores[:, :, None], axis=1)
    priority = slot_order[0]
    before = (priority[None, :] < priority[:, None]).astype(jnp.bfloat16)
    rank = jnp.dot(before, hit.astype(jnp.bfloat16), preferred_element_type=jnp.float32)
    counts = jnp.sum(hit, axis=0)
    every = lax.all_to_all(
        jnp.broadcast_to(counts[None, :], (experts, experts)), "ep", 0, 0, tiled=True
    )
    load = jnp.sum(every, axis=0)
    pairs = [(i, (i ^ 1) % groups) for i in range(groups)]
    load_there = lax.ppermute(load, "rep", pairs)
    earlier = (jnp.arange(experts) < ep_index).astype(jnp.float32)
    start = jnp.sum(every * earlier[:, None], axis=0)
    caps = capacity.astype(jnp.float32)
    pair = jnp.bitwise_xor(rep_index, 1) % groups
    cap_here = lax.dynamic_index_in_dim(caps, rep_index, 0, keepdims=False)
    cap_there = lax.dynamic_index_in_dim(caps, pair, 0, keepdims=False)
    limit = cap_here + jnp.minimum(jnp.maximum(cap_there - load_there, 0.0), SPILL)
    kept = hit * (start[None, :] + rank < limit[None, :]).astype(jnp.float32)
    kept_score = score * kept
    total = jnp.sum(gate_scores, axis=1)
    kept_sum = jnp.sum(kept_score, axis=1)
    weight = kept_score / jnp.maximum(kept_sum, 0.25 * total)[:, None]
    return weight.T


def spread_weights(weight_t, rows):
    experts = lax.axis_size("ep")
    me = lax.axis_index("ep")
    core, col, row = me % 2, (me // 2) % SIDE, me // (2 * SIDE)
    tok_rows = weight_t.shape[1]
    swapped = weight_t.reshape(experts // 2, 2, tok_rows)[:, ::-1].reshape(experts, tok_rows)
    sent = jnp.stack([weight_t, swapped], axis=1)
    got = lax.all_to_all(sent, "ep", 0, 0, tiled=True)
    got = got.reshape(SIDE, SIDE, 2, 2, tok_rows)
    mine = lax.dynamic_index_in_dim(got, core, 2, keepdims=False)
    mine = lax.dynamic_slice_in_dim(jnp.concatenate([mine, mine], 0), row, SIDE, 0)
    mine = lax.dynamic_slice_in_dim(jnp.concatenate([mine, mine], 1), col, SIDE, 1)
    mine = mine.reshape(SIDE, SIDE, 2, CHUNKS, 2, rows)
    first = mine[:, :, :, :, 0].transpose(3, 0, 1, 4, 2)
    second = mine[:, :, :, :, 1].transpose(3, 1, 0, 4, 2)
    both = jnp.stack([first, second], axis=2)
    return both.reshape(CHUNKS * SIDE, 2 * SIDE * rows, 2)


def kernel(
    tok, wt, wg, wu, wd,
    out, xg, rh, rf,
    wgv, wuv, wdv, xv, stg, total, hid, rv, st2, ph, pf,
    load_sem, own_sem, send_sem, recv_sem,
):
    me = lax.axis_index("ep")
    core, col, row = me % 2, (me // 2) % SIDE, me // (2 * SIDE)

    def at(r, c, k):
        return (r * SIDE + c) * 2 + k

    x_next, x_prev = at(row, (col + 1) % SIDE, core), at(row, (col + 3) % SIDE, core)
    z_next, z_prev = at((row + 1) % SIDE, col, core), at((row + 3) % SIDE, col, core)
    twin = at(row, col, 1 - core)
    near = ((x_next, x_prev), (z_next, z_prev))
    far = ((z_next, z_prev), (x_next, x_prev))

    depth = tok.shape[1]
    inner = wg.shape[1]
    rows = tok.shape[0] // (2 * CHUNKS)
    half = rows // 2
    group = SIDE * rows
    ghalf = group // 2
    ntile = min(256, inner)
    otile = min(512, depth)

    barrier = pltpu.get_barrier_semaphore()
    for dev in (x_next, x_prev, z_next, z_prev, twin):
        pl.semaphore_signal(barrier, inc=1, device_id={"ep": dev}, device_id_type=MESH)

    made = []

    def send(src, dst, dev):
        k = len(made)
        copy = pltpu.make_async_remote_copy(
            src_ref=src, dst_ref=dst, send_sem=send_sem.at[k], recv_sem=recv_sem.at[k],
            device_id={"ep": dev}, device_id_type=MESH,
        )
        copy.start()
        made.append(copy)
        return copy

    stage_in = pltpu.make_async_copy(tok, xv.at[pl.ds(0, tok.shape[0])], load_sem.at[0])
    stage_in.start()
    pl.semaphore_wait(barrier, 5)

    own = {}

    def start_own(c):
        for r in range(2):
            src = tok.at[pl.ds((2 * c + r) * rows, rows)]
            own[c, r, 0] = send(src, xg.at[c, r, 0, pl.ds(3 * rows, rows)], near[r][0])
            own[c, r, 1] = send(src, xg.at[c, r, 0, pl.ds(rows, rows)], near[r][1])

    relay = {}

    def start_relay(c):
        for r in range(2):
            own[c, r, 1].wait_recv()
            relay[c, r, 1] = send(
                xg.at[c, r, 0, pl.ds(rows, half)],
                xg.at[c, r, 0, pl.ds(2 * rows, half)], near[r][1],
            )
            own[c, r, 0].wait_recv()
            relay[c, r, 0] = send(
                xg.at[c, r, 0, pl.ds(3 * rows + half, half)],
                xg.at[c, r, 0, pl.ds(2 * rows + half, half)], near[r][0],
            )

    wide = {}

    def start_wide(c):
        for r in range(2):
            relay[c, r, 0].wait_recv()
            relay[c, r, 1].wait_recv()
        for part in range(2):
            for r in range(2):
                lo = pl.ds(part * ghalf, ghalf)
                hi = pl.ds((1 - part) * ghalf, ghalf)
                wide[c, r, 1, part] = send(xg.at[c, r, 0, lo], xg.at[c, r, 1, lo], far[r][1])
                wide[c, r, 0, part] = send(xg.at[c, r, 0, hi], xg.at[c, r, 3, hi], far[r][0])

    last = {}

    def start_last(c):
        for r in range(2):
            lo = pl.ds(0, ghalf)
            hi = pl.ds(ghalf, ghalf)
            wide[c, r, 1, 0].wait_recv()
            last[c, r, 1] = send(xg.at[c, r, 1, lo], xg.at[c, r, 2, lo], far[r][1])
            wide[c, r, 0, 0].wait_recv()
            last[c, r, 0] = send(xg.at[c, r, 3, hi], xg.at[c, r, 2, hi], far[r][0])

    def end_gather(c):
        for r in range(2):
            for k in range(2):
                wide[c, r, k, 1].wait_recv()
                last[c, r, k].wait_recv()

    start_own(0)
    weights = []
    for k, (src, dst) in enumerate(
        ((wg, wgv.at[:, pl.ds(0, inner)]), (wu, wuv.at[:, pl.ds(0, inner)]), (wd, wdv.at[pl.ds(0, inner)]))
    ):
        copy = pltpu.make_async_copy(src, dst, own_sem.at[k])
        copy.start()
        weights.append(copy)
    swaps = [
        send(wg, wgv.at[:, pl.ds(inner, inner)], twin),
        send(wu, wuv.at[:, pl.ds(inner, inner)], twin),
        send(wd, wdv.at[pl.ds(inner, inner)], twin),
    ]
    stage_in.wait()
    stage_out = []
    for c in range(CHUNKS):
        for r in range(2):
            copy = pltpu.make_async_copy(
                xv.at[pl.ds((2 * c + r) * rows, rows)],
                xg.at[c, r, 0, pl.ds(0, rows)], own_sem.at[3 + 2 * c + r],
            )
            copy.start()
            stage_out.append(copy)
    start_relay(0)
    start_own(1)
    for copy in stage_out:
        copy.wait()
    start_wide(0)
    start_relay(1)
    start_last(0)
    start_wide(1)
    for copy in weights:
        copy.wait()
    for copy in swaps:
        copy.wait_recv()
    end_gather(0)

    def fetch(c, d):
        copies = []
        for r in range(2):
            copy = pltpu.make_async_copy(
                xg.at[c, r, d], xv.at[pl.ds(r * group, group)], load_sem.at[r]
            )
            copy.start()
            copies.append(copy)
        return copies

    def up_phase(c, d):
        index = c * SIDE + d
        for e in range(2):
            scale = wt[index, :, e:e + 1]

            def tile(n, carry):
                cols = pl.ds(pl.multiple_of(e * inner + n * ntile, ntile), ntile)
                gate = jnp.dot(xv[...], wgv[:, cols], preferred_element_type=jnp.float32)
                up = jnp.dot(xv[...], wuv[:, cols], preferred_element_type=jnp.float32)
                hidden = gate / (1.0 + jnp.exp(-gate)) * up * scale
                hid[:, cols] = hidden.astype(jnp.bfloat16)
                return carry

            lax.fori_loop(0, inner // ntile, tile, 0)

    def down_phase(finish):
        def tile(n, carry):
            cols = pl.ds(pl.multiple_of(n * otile, otile), otile)
            finish(cols, jnp.dot(hid[...], wdv[:, cols], preferred_element_type=jnp.float32))
            return carry

        lax.fori_loop(0, depth // otile, tile, 0)

    def bring(pieces):
        copies = []
        for k, (src, dst) in enumerate(pieces):
            copy = pltpu.make_async_copy(src, dst, load_sem.at[2 + k])
            copy.start()
            copies.append(copy)
        for copy in copies:
            copy.wait()

    halves, fulls, near_h, near_f = {}, {}, {}, {}

    def reuse(sent, c, keys):
        if c > 0:
            for key in keys:
                sent[(c - 1,) + key].wait_send()

    def finish_two(c):
        reuse(halves, c, [(r, k) for r in range(2) for k in range(2)])

        def store(cols, part):
            stg[0, :, cols] = part.astype(jnp.bfloat16)

        down_phase(store)
        for r in range(2):
            halves[c, r, 0] = send(stg.at[0, pl.ds(r * group, ghalf)], rh.at[c, 0, r], far[r][0])
            halves[c, r, 1] = send(stg.at[0, pl.ds(r * group + ghalf, ghalf)], rh.at[c, 1, r], far[r][1])

    def finish_side(c, k):
        for r in range(2):
            halves[c, r, k].wait_recv()
        bring([(rh.at[c, k, r], rv.at[0, pl.ds(r * ghalf, ghalf)]) for r in range(2)])
        reuse(fulls, c, [(r, k) for r in range(2)])

        def store(cols, part):
            for r in range(2):
                with_it = r * group + k * ghalf
                alone = r * group + (1 - k) * ghalf
                added = part[with_it:with_it + ghalf] + rv[0, pl.ds(r * ghalf, ghalf), cols].astype(jnp.float32)
                stg[1 + k, pl.ds(with_it, ghalf), cols] = added.astype(jnp.bfloat16)
                stg[1 + k, pl.ds(alone, ghalf), cols] = part[alone:alone + ghalf].astype(jnp.bfloat16)

        down_phase(store)
        for r in range(2):
            fulls[c, r, k] = send(stg.at[1 + k, pl.ds(r * group, group)], rf.at[c, k, r], far[r][k])

    def finish_own(c):
        pieces = []
        for k in range(2):
            for r in range(2):
                fulls[c, r, k].wait_recv()
                pieces.append((rf.at[c, k, r], rv.at[k, pl.ds(r * group, group)]))
        bring(pieces)

        def store(cols, part):
            total[:, cols] = (
                part + rv[0, :, cols].astype(jnp.float32) + rv[1, :, cols].astype(jnp.float32)
            )

        down_phase(store)

    def near_start(c):
        reuse(near_h, c, [(r, k) for r in range(2) for k in range(2)])
        for r in range(2):
            st2[0, pl.ds(r * rows, rows)] = total[pl.ds(r * group + 2 * rows, rows)].astype(jnp.bfloat16)
        for r in range(2):
            near_h[c, r, 0] = send(st2.at[0, pl.ds(r * rows, half)], ph.at[c, 0, r], near[r][0])
            near_h[c, r, 1] = send(st2.at[0, pl.ds(r * rows + half, half)], ph.at[c, 1, r], near[r][1])

    def near_middle(c):
        reuse(near_f, c, [(r, k) for r in range(2) for k in range(2)])
        for k in range(2):
            for r in range(2):
                near_h[c, r, k].wait_recv()
                base = r * group + (1 + 2 * k) * rows
                with_it, alone = k * half, (1 - k) * half
                st2[1 + k, pl.ds(r * rows + with_it, half)] = (
                    total[pl.ds(base + with_it, half)] + ph[c, k, r].astype(jnp.float32)
                ).astype(jnp.bfloat16)
                st2[1 + k, pl.ds(r * rows + alone, half)] = total[pl.ds(base + alone, half)].astype(jnp.bfloat16)
                near_f[c, r, k] = send(st2.at[1 + k, pl.ds(r * rows, rows)], pf.at[c, k, r], near[r][k])

    def near_end(c):
        for r in range(2):
            for k in range(2):
                near_f[c, r, k].wait_recv()
            out[pl.ds((2 * c + r) * rows, rows)] = (
                total[pl.ds(r * group, rows)]
                + pf[c, 0, r].astype(jnp.float32)
                + pf[c, 1, r].astype(jnp.float32)
            ).astype(jnp.bfloat16)

    order = (2, 1, 3, 0)
    waiting = fetch(0, 2)
    for c in range(CHUNKS):
        for place, d in enumerate(order):
            for copy in waiting:
                copy.wait()
            up_phase(c, d)
            if c == 0 and place == 0:
                start_last(1)
            if place < 3:
                waiting = fetch(c, order[place + 1])
            elif c + 1 < CHUNKS:
                end_gather(c + 1)
                waiting = fetch(c + 1, order[0])
            if d == 2:
                finish_two(c)
                if c > 0:
                    near_middle(c - 1)
            elif d == 0:
                finish_own(c)
            else:
                finish_side(c, 0 if d == 1 else 1)
                if c > 0 and d == 1:
                    near_end(c - 1)
        near_start(c)
    near_middle(CHUNKS - 1)
    near_end(CHUNKS - 1)

    waited = set()
    for sent in (halves, fulls, near_h, near_f):
        for key, copy in sent.items():
            if key[0] < CHUNKS - 1:
                waited.add(id(copy))
    for copy in made:
        if id(copy) not in waited:
            copy.wait_send()


N_MESSAGES = CHUNKS * 36 + 3


def expert_layer(tokens, weights, w_gate, w_up, w_down):
    tok_rows, depth = tokens.shape
    inner = w_gate.shape[1]
    rows = tok_rows // (2 * CHUNKS)
    group = SIDE * rows
    unit = 2 * group
    bf16 = jnp.bfloat16
    hbm = pl.BlockSpec(memory_space=pl.ANY)
    vmem = pl.BlockSpec(memory_space=pltpu.VMEM)
    shapes = (
        jax.ShapeDtypeStruct((tok_rows, depth), bf16),
        jax.ShapeDtypeStruct((CHUNKS, 2, SIDE, group, depth), bf16),
        jax.ShapeDtypeStruct((CHUNKS, 2, 2, group // 2, depth), bf16),
        jax.ShapeDtypeStruct((CHUNKS, 2, 2, group, depth), bf16),
    )
    scratch = [
        pltpu.VMEM((depth, 2 * inner), bf16),
        pltpu.VMEM((depth, 2 * inner), bf16),
        pltpu.VMEM((2 * inner, depth), bf16),
        pltpu.VMEM((unit, depth), bf16),
        pltpu.VMEM((3, unit, depth), bf16),
        pltpu.VMEM((unit, depth), jnp.float32),
        pltpu.VMEM((unit, 2 * inner), bf16),
        pltpu.VMEM((2, unit, depth), bf16),
        pltpu.VMEM((3, 2 * rows, depth), bf16),
        pltpu.VMEM((CHUNKS, 2, 2, rows // 2, depth), bf16),
        pltpu.VMEM((CHUNKS, 2, 2, rows, depth), bf16),
        pltpu.SemaphoreType.DMA((6,)),
        pltpu.SemaphoreType.DMA((3 + 2 * CHUNKS,)),
        pltpu.SemaphoreType.DMA((N_MESSAGES,)),
        pltpu.SemaphoreType.DMA((N_MESSAGES,)),
    ]
    return pl.pallas_call(
        kernel,
        out_shape=shapes,
        in_specs=[hbm, vmem, hbm, hbm, hbm],
        out_specs=(vmem, hbm, hbm, hbm),
        scratch_shapes=scratch,
        compiler_params=pltpu.CompilerParams(
            collective_id=0, has_side_effects=True, vmem_limit_bytes=66 * 1000 * 1000
        ),
    )(tokens, weights, w_gate, w_up, w_down)[0]


def on_device(tokens, routes, gate_scores, slot_order, capacity, w_gate, w_up, w_down):
    weight_t = routing_weights(routes, gate_scores, slot_order, capacity)
    spread = spread_weights(weight_t, tokens.shape[0] // (2 * CHUNKS))
    return expert_layer(tokens, spread, w_gate[0], w_up[0], w_down[0])


def solution(mesh):
    placed = (
        P(("rep", "ep"), None),
        P(("rep", "ep"), None),
        P(("rep", "ep"), None),
        P(("rep", "ep"), None),
        P(),
        P("ep", None, None),
        P("ep", None, None),
        P("ep", None, None),
    )
    return jax.shard_map(
        on_device, mesh=mesh, in_specs=placed, out_specs=P(("rep", "ep"), None), check_vma=False
    )
```

time: 405 us -> 279 us (0.69)
  Pallas kernels: 0 us -> 241 us
  blocking collectives: 191 us -> 0 us
  waiting for transfers between devices: 133 us -> 15.1 us
  matrix products: 38.9 us -> 0.97 us
  local copies, waits for them, and re-layouts: 21.3 us -> 5.21 us
  other arithmetic: 15 us -> 2.46 us
  starting transfers between devices: 5.12 us -> 13.8 us
    pallas_call x0 -> x1, Pallas kernels: none -> 241 us  [expert_layer(): pl.pallas_call(kernel, out_shape=shapes, in_specs=[hbm, vmem, hbm, hbm, h...]
    all_to_all x1 -> x0, blocking collectives: 122 us -> none  [on_device(): lax.all_to_all(outgoing, 'ep', split_axis=0, concat_axis=0, tiled=True)]
    all_to_all x1 -> x2, waiting for transfers between devices: 133 us -> 13.2 us  [the longest x1 7.36 us: spread_weights(): got = lax.all_to_all(sent, 'ep', 0, 0, tiled=True)]
    unnamed x1 -> x0, blocking collectives: 68.2 us -> none
    dot_general x5 -> x1, matrix products: 38.9 us -> 0.97 us  [routing_weights(): jnp.dot(before, hit.astype(jnp.bfloat16), preferred_element_type=jnp.floa...]
    gather x1 -> x0, local copies, waits for them, and re-layouts: 20.5 us -> none  [on_device(): picked = returned.reshape(experts * SLOT, width)[row_index]]
    reduce_sum x6 -> x4, other arithmetic: 14 us -> 1.65 us  [the longest x1 0.84 us: routing_weights(): counts = jnp.sum(hit, axis=0)]
    all_to_all x1 -> x2, starting transfers between devices: 5.12 us -> 12.1 us  [the longest x1 8.27 us: routing_weights(): lax.all_to_all(jnp.broadcast_to(counts[None, :], (experts, experts)), 'ep...]
  transfers between devices with their start and end apart: 1 -> 3, of which waited for: 1 -> 3; matrix products, arithmetic and copies ran while one was open for 0% -> 1% of each run, Pallas kernels for 0% -> 0%
where the time goes in v2:
time: 279 us; the launch traced here: 278 us
  Pallas kernels  241 us (86%)
  waiting for transfers between devices  15.1 us (5%)
  starting transfers between devices  13.8 us (5%)
  local copies, waits for them, and re-layouts  5.21 us (2%)
    pallas_call x1, Pallas kernels, expert_layer(): pl.pallas_call(kernel, out_shape=shapes, in_specs=[hbm, vmem, hbm, hbm, h...  241 us
    all_to_all x1, starting transfers between devices, routing_weights(): lax.all_to_all(jnp.broadcast_to(counts[None, :], (experts, experts)), 'ep...  8.27 us
    all_to_all x1, waiting for transfers between devices, spread_weights(): got = lax.all_to_all(sent, 'ep', 0, 0, tiled=True)  7.36 us
    all_to_all x1, waiting for transfers between devices, routing_weights(): lax.all_to_all(jnp.broadcast_to(counts[None, :], (experts, experts)), 'ep...  5.88 us
  transfers between devices with their start and end apart: 3, of which 3 were waited for; matrix products, arithmetic and copies ran while one was open for 1% of the time, Pallas kernels for 0%

profile of v2, /device:TPU:0, one launch (start us, length us, event | category | flops | bytes accessed | tf_op | source)
XLA Modules:
  0.0 278.3 jit_solution(11430702096749093976)
XLA Ops:
  0.0 0.8 convert_reduce_fusion.1
  0.8 0.6 broadcast_in_dim.2
  1.5 8.3 %all-to-all-start = ((f32[32,1,32]{2,1,0:T(1,128)}), f32[32,1,32]{2,1,0:T(1,128)S(1)}, u32[]{:S(2)}, u32[]{:S(2)}) async-start(f32[32,1,32]{2,1,0:T(1,128)} %broadcast_in_dim.2), calls=%async_computation | async-start | bytes 32768 | tf_op jit(solution)/shard_map/all_to_all | solution.py:29
  9.8 0.7 reduce_sum.69
  10.5 0.7 convert_element_type.21
  11.2 5.9 %all-to-all-done = f32[32,1,32]{2,1,0:T(1,128)S(1)} async-done(((f32[32,1,32]{2,1,0:T(1,128)}), f32[32,1,32]{2,1,0:T(1,128)S(1)}, u32[]{:S(2)}, u32[]{:S(2)}) %all-to-all-start) | async-done | bytes 4128 | tf_op jit(solution)/shard_map/all_to_all | solution.py:29
  17.1 1.6 collective-permute-start
  18.7 0.1 multiply_reduce_fusion
  18.8 1.9 collective-permute-done
  20.7 1.0 fusion.16
  21.8 0.6 copy.26
  22.4 3.9 %all-to-all-start.1 = ((f32[32,2,128]{2,1,0:T(2,128)}), f32[32,2,128]{2,1,0:T(2,128)S(1)}, u32[]{:S(2)}, u32[]{:S(2)}) async-start(f32[32,2,128]{2,1,0:T(2,128)} %copy.26), calls=%async_computation.1 | async-start | bytes 65536 | tf_op jit(solution)/shard_map/all_to_all | solution.py:57
  26.3 7.4 %all-to-all-done.1 = f32[32,2,128]{2,1,0:T(2,128)S(1)} async-done(((f32[32,2,128]{2,1,0:T(2,128)}), f32[32,2,128]{2,1,0:T(2,128)S(1)}, u32[]{:S(2)}, u32[]{:S(2)}) %all-to-all-start.1) | async-done | bytes 32800 | tf_op jit(solution)/shard_map/all_to_all | solution.py:57
  33.8 0.1 reshape.36
  33.9 0.1 fusion.15
  34.0 1.4 copy.28
  35.5 240.6 %shard_map.82 = (bf16[128,4096]{1,0:T(8,128)(2,1)}, bf16[2,2,4,128,4096]{4,3,2,1,0:T(8,128)(2,1)}, bf16[2,2,2,64,4096]{4,3,2,1,0:T(8,128)(2,1)}, bf16[2,2,2,128,4096]{4,3,2,1,0:T(8,128)(2,1)}) custom-call(bf16[128,4096]{1,0:T(8,128)(2,1)} %tok.1, f32[8,256,2]{2,1,0:T(8,128)} %bitcast.44, bf16[4096,768]{1,0:T(8,128)(2,1)} %bitcast.41, ...), custom_call_target="tpu_custom_call" | custom-call | tf_op jit(solution)/shard_map/pallas_call | solution.py:403
  276.0 2.3 copy.33
  (13 shorter events, 0.2 us)
Async XLA Ops:
  1.5 15.6 %all-to-all-start = ((f32[32,1,32]{2,1,0:T(1,128)}), f32[32,1,32]{2,1,0:T(1,128)S(1)}, u32[]{:S(2)}, u32[]{:S(2)}) async-start(f32[32,1,32]{2,1,0:T(1,128)} %broadcast_in_dim.2), calls=%async_computation | async-start | bytes 32768 | tf_op jit(solution)/shard_map/all_to_all | solution.py:29
  17.1 3.6 %collective-permute-start = (f32[32]{0:T(128)S(1)}, f32[32]{0:T(128)S(1)}, u32[]{:S(2)}, u32[]{:S(2)}) collective-permute-start(f32[32]{0:T(128)S(1)} %reduce_sum.67), channel_id=1, source_target_pairs={{0,32},{32,0},{64,96},{96,64},{1,33},{33,1},{65,97},{97,65},{2,34}... | collective-permute-start | bytes 392 | tf_op jit(solution)/shard_map/ppermute | solution.py:34
  22.4 11.3 %all-to-all-start.1 = ((f32[32,2,128]{2,1,0:T(2,128)}), f32[32,2,128]{2,1,0:T(2,128)S(1)}, u32[]{:S(2)}, u32[]{:S(2)}) async-start(f32[32,2,128]{2,1,0:T(2,128)} %copy.26), calls=%async_computation.1 | async-start | bytes 65536 | tf_op jit(solution)/shard_map/all_to_all | solution.py:57

commit v3 on v2

--- a/solution.py
+++ b/solution.py
@@ -68,9 +68,9 @@
 
 def kernel(
     tok, wt, wg, wu, wd,
-    out, xg, rh, rf,
-    wgv, wuv, wdv, xv, stg, total, hid, rv, st2, ph, pf,
-    load_sem, own_sem, send_sem, recv_sem,
+    out, xg, rh, rf, part,
+    wgv, wuv, wdv, xv, stg, mix, total, hid, rv, st2, ph, pf,
+    load_sem, own_sem, put_sem, send_sem, recv_sem,
 ):
     me = lax.axis_index("ep")
     core, col, row = me % 2, (me // 2) % SIDE, me // (2 * SIDE)
@@ -228,13 +228,27 @@
 
             lax.fori_loop(0, inner // ntile, tile, 0)
 
-    def down_phase(finish):
+    def down_phase(c, d, slot):
+        def put(n):
+            cols = pl.ds(pl.multiple_of(n * otile, otile), otile)
+            pltpu.make_async_copy(
+                stg.at[slot, :, cols], part.at[c, d, :, cols], put_sem.at[slot]
+            ).start()
+
         def tile(n, carry):
             cols = pl.ds(pl.multiple_of(n * otile, otile), otile)
-            finish(cols, jnp.dot(hid[...], wdv[:, cols], preferred_element_type=jnp.float32))
+            value = jnp.dot(hid[...], wdv[:, cols], preferred_element_type=jnp.float32)
+            stg[slot, :, cols] = value.astype(jnp.bfloat16)
+
+            @pl.when(n > 0)
+            def _():
+                put(n - 1)
+
             return carry
 
         lax.fori_loop(0, depth // otile, tile, 0)
+        put(depth // otile - 1)
+        pltpu.make_async_copy(stg.at[slot], part.at[c, d], put_sem.at[slot]).wait()
 
     def bring(pieces):
         copies = []
@@ -245,56 +259,66 @@
         for copy in copies:
             copy.wait()
 
-    halves, fulls, near_h, near_f = {}, {}, {}, {}
+    halves, alones, fulls, near_h, near_f = {}, {}, {}, {}, {}
 
     def reuse(sent, c, keys):
         if c > 0:
             for key in keys:
                 sent[(c - 1,) + key].wait_send()
 
-    def finish_two(c):
-        reuse(halves, c, [(r, k) for r in range(2) for k in range(2)])
-
-        def store(cols, part):
-            stg[0, :, cols] = part.astype(jnp.bfloat16)
-
-        down_phase(store)
-        for r in range(2):
-            halves[c, r, 0] = send(stg.at[0, pl.ds(r * group, ghalf)], rh.at[c, 0, r], far[r][0])
-            halves[c, r, 1] = send(stg.at[0, pl.ds(r * group + ghalf, ghalf)], rh.at[c, 1, r], far[r][1])
-
-    def finish_side(c, k):
-        for r in range(2):
-            halves[c, r, k].wait_recv()
-        bring([(rh.at[c, k, r], rv.at[0, pl.ds(r * ghalf, ghalf)]) for r in range(2)])
-        reuse(fulls, c, [(r, k) for r in range(2)])
-
-        def store(cols, part):
-            for r in range(2):
-                with_it = r * group + k * ghalf
-                alone = r * group + (1 - k) * ghalf
-                added = part[with_it:with_it + ghalf] + rv[0, pl.ds(r * ghalf, ghalf), cols].astype(jnp.float32)
-                stg[1 + k, pl.ds(with_it, ghalf), cols] = added.astype(jnp.bfloat16)
-                stg[1 + k, pl.ds(alone, ghalf), cols] = part[alone:alone + ghalf].astype(jnp.bfloat16)
-
-        down_phase(store)
-        for r in range(2):
-            fulls[c, r, k] = send(stg.at[1 + k, pl.ds(r * group, group)], rf.at[c, k, r], far[r][k])
-
-    def finish_own(c):
+    def far_halves(c):
+        for r in range(2):
+            halves[c, r, 0] = send(part.at[c, 2, pl.ds(r * group, ghalf)], rh.at[c, 0, r], far[r][0])
+            halves[c, r, 1] = send(part.at[c, 2, pl.ds(r * group + ghalf, ghalf)], rh.at[c, 1, r], far[r][1])
+
+    def far_alone(c, k):
+        for r in range(2):
+            alone = (1 - k) * ghalf
+            src = part.at[c, 1 + 2 * k, pl.ds(r * group + alone, ghalf)]
+            alones[c, r, k] = send(src, rf.at[c, k, r, pl.ds(alone, ghalf)], far[r][k])
+
+    def far_sum(c):
+        reuse(fulls, c, [(r, k) for r in range(2) for k in range(2)])
         pieces = []
         for k in range(2):
             for r in range(2):
+                halves[c, r, k].wait_recv()
+                to = pl.ds((2 * k + r) * ghalf, ghalf)
+                pieces.append((rh.at[c, k, r], rv.at[0, to]))
+                pieces.append((part.at[c, 1 + 2 * k, pl.ds(r * group + k * ghalf, ghalf)], rv.at[1, to]))
+        bring(pieces)
+
+        def tile(n, carry):
+            cols = pl.ds(pl.multiple_of(n * otile, otile), otile)
+            added = rv[0, :, cols].astype(jnp.float32) + rv[1, :, cols].astype(jnp.float32)
+            mix[:, cols] = added.astype(jnp.bfloat16)
+            return carry
+
+        lax.fori_loop(0, depth // otile, tile, 0)
+        for k in range(2):
+            for r in range(2):
+                src = mix.at[pl.ds((2 * k + r) * ghalf, ghalf)]
+                fulls[c, r, k] = send(src, rf.at[c, k, r, pl.ds(k * ghalf, ghalf)], far[r][k])
+
+    def own_sum(c):
+        pieces = [(part.at[c, 0], stg.at[0])]
+        for k in range(2):
+            for r in range(2):
+                alones[c, r, k].wait_recv()
                 fulls[c, r, k].wait_recv()
                 pieces.append((rf.at[c, k, r], rv.at[k, pl.ds(r * group, group)]))
         bring(pieces)
 
-        def store(cols, part):
+        def tile(n, carry):
+            cols = pl.ds(pl.multiple_of(n * otile, otile), otile)
             total[:, cols] = (
-                part + rv[0, :, cols].astype(jnp.float32) + rv[1, :, cols].astype(jnp.float32)
+                stg[0, :, cols].astype(jnp.float32)
+                + rv[0, :, cols].astype(jnp.float32)
+                + rv[1, :, cols].astype(jnp.float32)
             )
-
-        down_phase(store)
+            return carry
+
+        lax.fori_loop(0, depth // otile, tile, 0)
 
     def near_start(c):
         reuse(near_h, c, [(r, k) for r in range(2) for k in range(2)])
@@ -341,22 +365,32 @@
             elif c + 1 < CHUNKS:
                 end_gather(c + 1)
                 waiting = fetch(c + 1, order[0])
+            down_phase(c, d, 1)
             if d == 2:
-                finish_two(c)
+                far_halves(c)
+            elif d == 1:
+                far_alone(c, 0)
+                if c > 0:
+                    own_sum(c - 1)
+                    near_start(c - 1)
+            elif d == 3:
+                far_alone(c, 1)
                 if c > 0:
                     near_middle(c - 1)
-            elif d == 0:
-                finish_own(c)
+                if c == CHUNKS - 1:
+                    far_sum(c)
+            elif c > 0:
+                near_end(c - 1)
             else:
-                finish_side(c, 0 if d == 1 else 1)
-                if c > 0 and d == 1:
-                    near_end(c - 1)
-        near_start(c)
-    near_middle(CHUNKS - 1)
-    near_end(CHUNKS - 1)
+                far_sum(c)
+    last_chunk = CHUNKS - 1
+    own_sum(last_chunk)
+    near_start(last_chunk)
+    near_middle(last_chunk)
+    near_end(last_chunk)
 
     waited = set()
-    for sent in (halves, fulls, near_h, near_f):
+    for sent in (fulls, near_h, near_f):
         for key, copy in sent.items():
             if key[0] < CHUNKS - 1:
                 waited.add(id(copy))
@@ -365,7 +399,7 @@
             copy.wait_send()
 
 
-N_MESSAGES = CHUNKS * 36 + 3
+N_MESSAGES = CHUNKS * 40 + 3
 
 
 def expert_layer(tokens, weights, w_gate, w_up, w_down):
@@ -382,21 +416,24 @@
         jax.ShapeDtypeStruct((CHUNKS, 2, SIDE, group, depth), bf16),
         jax.ShapeDtypeStruct((CHUNKS, 2, 2, group // 2, depth), bf16),
         jax.ShapeDtypeStruct((CHUNKS, 2, 2, group, depth), bf16),
+        jax.ShapeDtypeStruct((CHUNKS, SIDE, unit, depth), bf16),
     )
     scratch = [
         pltpu.VMEM((depth, 2 * inner), bf16),
         pltpu.VMEM((depth, 2 * inner), bf16),
         pltpu.VMEM((2 * inner, depth), bf16),
         pltpu.VMEM((unit, depth), bf16),
-        pltpu.VMEM((3, unit, depth), bf16),
+        pltpu.VMEM((2, unit, depth), bf16),
+        pltpu.VMEM((unit, depth), bf16),
         pltpu.VMEM((unit, depth), jnp.float32),
         pltpu.VMEM((unit, 2 * inner), bf16),
         pltpu.VMEM((2, unit, depth), bf16),
         pltpu.VMEM((3, 2 * rows, depth), bf16),
         pltpu.VMEM((CHUNKS, 2, 2, rows // 2, depth), bf16),
         pltpu.VMEM((CHUNKS, 2, 2, rows, depth), bf16),
-        pltpu.SemaphoreType.DMA((6,)),
+        pltpu.SemaphoreType.DMA((10,)),
         pltpu.SemaphoreType.DMA((3 + 2 * CHUNKS,)),
+        pltpu.SemaphoreType.DMA((2,)),
         pltpu.SemaphoreType.DMA((N_MESSAGES,)),
         pltpu.SemaphoreType.DMA((N_MESSAGES,)),
     ]
@@ -404,7 +441,7 @@
         kernel,
         out_shape=shapes,
         in_specs=[hbm, vmem, hbm, hbm, hbm],
-        out_specs=(vmem, hbm, hbm, hbm),
+        out_specs=(vmem, hbm, hbm, hbm, hbm),
         scratch_shapes=scratch,
         compiler_params=pltpu.CompilerParams(
             collective_id=0, has_side_effects=True, vmem_limit_bytes=66 * 1000 * 1000

time: 279 us -> 246 us (0.88)
  Pallas kernels: 241 us -> 208 us
    pallas_call x1, Pallas kernels: 241 us -> 208 us  [expert_layer(): pl.pallas_call(kernel, out_shape=shapes, in_specs=[hbm, vmem, hbm, hbm, h...]
where the time goes in v3:
time: 246 us
  Pallas kernels  208 us (85%)
  waiting for transfers between devices  15.1 us (6%)
  starting transfers between devices  13.8 us (6%)
  local copies, waits for them, and re-layouts  5.21 us (2%)
  other arithmetic  2.46 us (1%)
    pallas_call x1, Pallas kernels, expert_layer(): pl.pallas_call(kernel, out_shape=shapes, in_specs=[hbm, vmem, hbm, hbm, h...  208 us
    all_to_all x1, starting transfers between devices, routing_weights(): lax.all_to_all(jnp.broadcast_to(counts[None, :], (experts, experts)), 'ep...  8.27 us
    all_to_all x1, waiting for transfers between devices, spread_weights(): got = lax.all_to_all(sent, 'ep', 0, 0, tiled=True)  7.36 us
    all_to_all x1, waiting for transfers between devices, routing_weights(): lax.all_to_all(jnp.broadcast_to(counts[None, :], (experts, experts)), 'ep...  5.88 us
  transfers between devices with their start and end apart: 3, of which 3 were waited for; matrix products, arithmetic and copies ran while one was open for 1% of the time, Pallas kernels for 0%

profile of v3, /device:TPU:0, one launch (start us, length us, event | category | flops | bytes accessed | tf_op | source)
XLA Modules:
  0.0 245.9 jit_solution(8482476909904754412)
XLA Ops:
  0.0 0.8 convert_reduce_fusion.1
  0.8 0.6 broadcast_in_dim.2
  1.5 8.3 %all-to-all-start = ((f32[32,1,32]{2,1,0:T(1,128)}), f32[32,1,32]{2,1,0:T(1,128)S(1)}, u32[]{:S(2)}, u32[]{:S(2)}) async-start(f32[32,1,32]{2,1,0:T(1,128)} %broadcast_in_dim.2), calls=%async_computation | async-start | bytes 32768 | tf_op jit(solution)/shard_map/all_to_all | solution.py:29
  9.8 0.7 reduce_sum.69
  10.5 0.7 convert_element_type.21
  11.2 5.9 %all-to-all-done = f32[32,1,32]{2,1,0:T(1,128)S(1)} async-done(((f32[32,1,32]{2,1,0:T(1,128)}), f32[32,1,32]{2,1,0:T(1,128)S(1)}, u32[]{:S(2)}, u32[]{:S(2)}) %all-to-all-start) | async-done | bytes 4128 | tf_op jit(solution)/shard_map/all_to_all | solution.py:29
  17.1 1.6 collective-permute-start
  18.7 0.1 multiply_reduce_fusion
  18.8 1.9 collective-permute-done
  20.7 1.0 fusion.16
  21.8 0.6 copy.26
  22.4 3.9 %all-to-all-start.1 = ((f32[32,2,128]{2,1,0:T(2,128)}), f32[32,2,128]{2,1,0:T(2,128)S(1)}, u32[]{:S(2)}, u32[]{:S(2)}) async-start(f32[32,2,128]{2,1,0:T(2,128)} %copy.26), calls=%async_computation.1 | async-start | bytes 65536 | tf_op jit(solution)/shard_map/all_to_all | solution.py:57
  26.3 7.4 %all-to-all-done.1 = f32[32,2,128]{2,1,0:T(2,128)S(1)} async-done(((f32[32,2,128]{2,1,0:T(2,128)}), f32[32,2,128]{2,1,0:T(2,128)S(1)}, u32[]{:S(2)}, u32[]{:S(2)}) %all-to-all-start.1) | async-done | bytes 32800 | tf_op jit(solution)/shard_map/all_to_all | solution.py:57
  33.8 0.1 reshape.36
  33.9 0.1 fusion.15
  34.0 1.4 copy.28
  35.5 208.2 %shard_map.82 = (bf16[128,4096]{1,0:T(8,128)(2,1)}, bf16[2,2,4,128,4096]{4,3,2,1,0:T(8,128)(2,1)}, bf16[2,2,2,64,4096]{4,3,2,1,0:T(8,128)(2,1)}, bf16[2,2,2,128,...) custom-call(bf16[128,4096]{1,0:T(8,128)(2,1)} %tok.1, f32[8,256,2]{2,1,0:T(8,128)} %bitcast.44, ...), custom_call_target="tpu_custom_call" | custom-call | tf_op jit(solution)/shard_map/pallas_call | solution.py:440
  243.6 2.3 copy.33
  (13 shorter events, 0.2 us)
Async XLA Ops:
  1.5 15.6 %all-to-all-start = ((f32[32,1,32]{2,1,0:T(1,128)}), f32[32,1,32]{2,1,0:T(1,128)S(1)}, u32[]{:S(2)}, u32[]{:S(2)}) async-start(f32[32,1,32]{2,1,0:T(1,128)} %broadcast_in_dim.2), calls=%async_computation | async-start | bytes 32768 | tf_op jit(solution)/shard_map/all_to_all | solution.py:29
  17.1 3.6 %collective-permute-start = (f32[32]{0:T(128)S(1)}, f32[32]{0:T(128)S(1)}, u32[]{:S(2)}, u32[]{:S(2)}) collective-permute-start(f32[32]{0:T(128)S(1)} %reduce_sum.67), channel_id=1, source_target_pairs={{0,32},{32,0},{64,96},{96,64},{1,33},{33,1},{65,97},{97,65},{2,34}... | collective-permute-start | bytes 392 | tf_op jit(solution)/shard_map/ppermute | solution.py:34
  22.4 11.3 %all-to-all-start.1 = ((f32[32,2,128]{2,1,0:T(2,128)}), f32[32,2,128]{2,1,0:T(2,128)S(1)}, u32[]{:S(2)}, u32[]{:S(2)}) async-start(f32[32,2,128]{2,1,0:T(2,128)} %copy.26), calls=%async_computation.1 | async-start | bytes 65536 | tf_op jit(solution)/shard_map/all_to_all | solution.py:57
